TPU v7x, 32 devices: a whole 2x2x4 slice. The times are simulated.
32 devices in a mesh: items: 8 (over y, x, core), seq: 4 (over z).
Axes of the slice: x: 2, y: 2, z: 4, core: 2. Of those that a mesh axis runs over, the one named last changes fastest.
Arguments:
- tokens: bfloat16 [24, 400, 768], P('items', 'seq'), may hold values from -6 to 6
- cotangent: bfloat16 [24, 400, 768], P('items', 'seq'), may hold values from -6 to 6
- ln1_gain: bfloat16 [768], replicated, may hold values from 0.099609375 to 1.8984375
- ln1_shift: bfloat16 [768], replicated, may hold values from -3 to 3
- w_query: bfloat16 [768, 768], replicated, may hold values from -0.21875 to 0.21875
- b_query: bfloat16 [768], replicated, may hold values from -3 to 3
- w_key: bfloat16 [768, 768], replicated, may hold values from -0.21875 to 0.21875
- w_value: bfloat16 [768, 768], replicated, may hold values from -0.21875 to 0.21875
- b_value: bfloat16 [768], replicated, may hold values from -3 to 3
- w_out: bfloat16 [768, 768], replicated, may hold values from -3.5 to 3.5
- b_out: bfloat16 [768], replicated, may hold values from -3 to 3
- ln2_gain: bfloat16 [768], replicated, may hold values from 0.099609375 to 1.8984375
- ln2_shift: bfloat16 [768], replicated, may hold values from -3 to 3
- w_inner: bfloat16 [768, 3072], replicated, may hold values from -0.21875 to 0.21875
- b_inner: bfloat16 [3072], replicated, may hold values from -3 to 3
- w_outer: bfloat16 [3072, 768], replicated, may hold values from -0.109375 to 0.109375
- b_outer: bfloat16 [768], replicated, may hold values from -3 to 3
- key_valid: int32 [24, 400], P('items'), may hold values from 0 to 1, as said below
Outputs:
- out_tokens: bfloat16 [24, 400, 768], P('items', 'seq')
- grad_tokens: bfloat16 [24, 400, 768], P('items', 'seq')
- grad_ln1_gain: float32 [768], replicated
- grad_ln1_shift: float32 [768], replicated
- grad_w_query: float32 [768, 768], replicated
- grad_b_query: float32 [768], replicated
- grad_w_key: float32 [768, 768], replicated
- grad_w_value: float32 [768, 768], replicated
- grad_b_value: float32 [768], replicated
- grad_w_out: float32 [768, 768], replicated
- grad_b_out: float32 [768], replicated
- grad_ln2_gain: float32 [768], replicated
- grad_ln2_shift: float32 [768], replicated
- grad_w_inner: float32 [768, 3072], replicated
- grad_b_inner: float32 [3072], replicated
- grad_w_outer: float32 [3072, 768], replicated
- grad_b_outer: float32 [768], replicated
Inputs may be any that keep to these rules, and one draw needn't show every extreme that they name: `key_valid`: in each item the ones come first and the zeros last; an item has 1 to 3 zeros, and some item has exactly 3.
All inputs are finite; a program needn't handle non-finite values.
Results may differ from a plain program's by a relative error of at most 0.012.
The roundings to bfloat16 on the way count: a program that leaves them out, or rounds other values in their place, can miss the bound.
Values may be sent and summed in bfloat16 or wider, within the bound.
No kernel may reach another device: no remote copies, remote signals or barrier semaphores. Data moves between devices by JAX's collectives and lax.ppermute only.
A program may use at most 192 MiB of HBM per device.

v0:
```python
import jax
import jax.numpy as jnp
from jax import lax
from jax.sharding import PartitionSpec as P

D = 768
HEADS = 12
HEAD_DIM = 64
FF = 3072
EPSILON = 1e-06
MASKED = -1000000000.0


def norm_rows(values, gain, shift):
    center = values - jnp.mean(values, axis=-1, keepdims=True)
    spread = jnp.mean(center * center, axis=-1, keepdims=True)
    return center * lax.rsqrt(spread + EPSILON) * gain + shift


def gelu_exact(values):
    return jax.nn.gelu(values, approximate=False)


def flat_rows(values):
    return values.reshape(-1, values.shape[-1])


def tall_dot(left, right):
    return jnp.einsum(
        "ti,tj->ij", flat_rows(left), flat_rows(right), preferred_element_type=jnp.float32
    )


def wide_dot(left, weight):
    return jnp.dot(flat_rows(left), weight, preferred_element_type=jnp.float32)


def back_dot(grads, weight):
    return jnp.einsum("tj,ij->ti", flat_rows(grads), weight, preferred_element_type=jnp.float32)


def column_sum(values):
    return jnp.sum(flat_rows(values.astype(jnp.float32)), axis=0)


def attend_scores(queries, keysets, usable, factor):
    scores = (
        jnp.einsum("bqhd,bkhd->bhqk", queries, keysets, preferred_element_type=jnp.float32) * factor
    )
    return jnp.where(usable[:, None, None, :] > 0, scores, MASKED)


def local(
    tokens,
    cotangent,
    ln1_gain,
    ln1_shift,
    w_query,
    b_query,
    w_key,
    w_value,
    b_value,
    w_out,
    b_out,
    ln2_gain,
    ln2_shift,
    w_inner,
    b_inner,
    w_outer,
    b_outer,
    key_valid,
):
    groups = lax.axis_size("seq")
    item_count, row_count, model_width = tokens.shape
    length = row_count * groups
    heads_here = HEADS // groups
    factor = HEAD_DIM ** (-0.5)
    token_shape = (item_count, row_count, model_width)
    head_shape = (item_count, length, heads_here, HEAD_DIM)
    inputs = tokens.astype(jnp.float32)
    normed, first_pull = jax.vjp(
        norm_rows, inputs, ln1_gain.astype(jnp.float32), ln1_shift.astype(jnp.float32)
    )
    normed_low = normed.astype(jnp.bfloat16)
    query = (
        (wide_dot(normed_low, w_query) + b_query.astype(jnp.float32))
        .astype(jnp.bfloat16)
        .reshape(token_shape)
    )
    keyset = wide_dot(normed_low, w_key).astype(jnp.bfloat16).reshape(token_shape)
    values = (
        (wide_dot(normed_low, w_value) + b_value.astype(jnp.float32))
        .astype(jnp.bfloat16)
        .reshape(token_shape)
    )
    query_heads, key_heads, value_heads = (
        lax.all_to_all(query, "seq", split_axis=2, concat_axis=1, tiled=True),
        lax.all_to_all(keyset, "seq", split_axis=2, concat_axis=1, tiled=True),
        lax.all_to_all(values, "seq", split_axis=2, concat_axis=1, tiled=True),
    )
    query_four = query_heads.reshape(head_shape)
    key_four = key_heads.reshape(head_shape)
    value_four = value_heads.reshape(head_shape)
    scores = attend_scores(query_four, key_four, key_valid, factor)
    row_top = jnp.max(scores, axis=-1, keepdims=True)
    weights = jnp.exp(scores - row_top)
    totals = jnp.sum(weights, axis=-1, keepdims=True)
    logsum = row_top + jnp.log(totals)
    probs_low = (weights / totals).astype(jnp.bfloat16)
    mixed = jnp.einsum("bhqk,bkhd->bqhd", probs_low, value_four, preferred_element_type=jnp.float32)
    mixed = mixed.astype(jnp.bfloat16).reshape(item_count, length, heads_here * HEAD_DIM)
    mixed_tokens = lax.all_to_all(mixed, "seq", split_axis=1, concat_axis=2, tiled=True)
    hidden = inputs + wide_dot(mixed_tokens, w_out).reshape(token_shape) + b_out.astype(jnp.float32)
    normed_two, second_pull = jax.vjp(
        norm_rows, hidden, ln2_gain.astype(jnp.float32), ln2_shift.astype(jnp.float32)
    )
    normed_two_low = normed_two.astype(jnp.bfloat16)
    inner = (wide_dot(normed_two_low, w_inner) + b_inner.astype(jnp.float32)).reshape(
        item_count, row_count, FF
    )
    active, gelu_pull = jax.vjp(gelu_exact, inner)
    active_low = active.astype(jnp.bfloat16)
    result = (
        hidden + wide_dot(active_low, w_outer).reshape(token_shape) + b_outer.astype(jnp.float32)
    )
    out_tokens = result.astype(jnp.bfloat16)
    grad_w_outer = tall_dot(active_low, cotangent)
    grad_b_outer = column_sum(cotangent)
    d_active = back_dot(cotangent, w_outer).reshape(item_count, row_count, FF)
    (d_inner,) = gelu_pull(d_active)
    d_inner_low = d_inner.astype(jnp.bfloat16)
    grad_w_inner = tall_dot(normed_two_low, d_inner_low)
    grad_b_inner = column_sum(d_inner_low)
    d_normed_two = back_dot(d_inner_low, w_inner).reshape(token_shape)
    d_hidden_part, grad_ln2_gain, grad_ln2_shift = second_pull(d_normed_two)
    d_hidden = cotangent.astype(jnp.float32) + d_hidden_part
    grad_b_out = column_sum(d_hidden)
    d_hidden_low = d_hidden.astype(jnp.bfloat16)
    grad_w_out = tall_dot(mixed_tokens, d_hidden_low)
    d_mixed = back_dot(d_hidden_low, w_out).astype(jnp.bfloat16).reshape(token_shape)
    d_mixed_heads = lax.all_to_all(d_mixed, "seq", split_axis=2, concat_axis=1, tiled=True)
    d_mixed_four = d_mixed_heads.reshape(head_shape)
    scores = attend_scores(query_four, key_four, key_valid, factor)
    probs = jnp.exp(scores - logsum)
    d_value = jnp.einsum(
        "bhqk,bqhd->bkhd",
        probs.astype(jnp.bfloat16),
        d_mixed_four,
        preferred_element_type=jnp.float32,
    )
    d_probs = jnp.einsum(
        "bqhd,bkhd->bhqk", d_mixed_four, value_four, preferred_element_type=jnp.float32
    )
    weighted = jnp.sum(probs * d_probs, axis=-1, keepdims=True)
    d_scores = (probs * (d_probs - weighted)).astype(jnp.bfloat16)
    d_query = (
        jnp.einsum("bhqk,bkhd->bqhd", d_scores, key_four, preferred_element_type=jnp.float32)
        * factor
    )
    d_key = (
        jnp.einsum("bhqk,bqhd->bkhd", d_scores, query_four, preferred_element_type=jnp.float32)
        * factor
    )
    flat_shape = (item_count, length, heads_here * HEAD_DIM)
    d_query = d_query.astype(jnp.bfloat16).reshape(flat_shape)
    d_key = d_key.astype(jnp.bfloat16).reshape(flat_shape)
    d_value = d_value.astype(jnp.bfloat16).reshape(flat_shape)
    d_query_tok, d_key_tok, d_value_tok = (
        lax.all_to_all(d_query, "seq", split_axis=1, concat_axis=2, tiled=True),
        lax.all_to_all(d_key, "seq", split_axis=1, concat_axis=2, tiled=True),
        lax.all_to_all(d_value, "seq", split_axis=1, concat_axis=2, tiled=True),
    )
    grad_w_query = tall_dot(normed_low, d_query_tok)
    grad_b_query = column_sum(d_query_tok)
    grad_w_key = tall_dot(normed_low, d_key_tok)
    grad_w_value = tall_dot(normed_low, d_value_tok)
    grad_b_value = column_sum(d_value_tok)
    d_normed = (
        back_dot(d_query_tok, w_query) + back_dot(d_key_tok, w_key) + back_dot(d_value_tok, w_value)
    )
    d_input_part, grad_ln1_gain, grad_ln1_shift = first_pull(d_normed.reshape(token_shape))
    grad_tokens = (d_hidden + d_input_part).astype(jnp.bfloat16)
    smalls = jnp.concatenate(
        [
            grad_ln1_gain,
            grad_ln1_shift,
            grad_b_query,
            grad_b_value,
            grad_b_out,
            grad_ln2_gain,
            grad_ln2_shift,
            grad_b_outer,
            grad_b_inner,
        ]
    )
    flat_query = grad_w_query.reshape(-1)
    flat_key = grad_w_key.reshape(-1)
    flat_value = grad_w_value.reshape(-1)
    flat_out = grad_w_out.reshape(-1)
    flat_inner = grad_w_inner.reshape(-1)
    flat_outer = grad_w_outer.reshape(-1)
    shares = (
        lax.psum_scatter(flat_query, ("items", "seq"), scatter_dimension=0, tiled=True),
        lax.psum_scatter(flat_key, ("items", "seq"), scatter_dimension=0, tiled=True),
        lax.psum_scatter(flat_value, ("items", "seq"), scatter_dimension=0, tiled=True),
        lax.psum_scatter(flat_out, ("items", "seq"), scatter_dimension=0, tiled=True),
        lax.psum_scatter(flat_inner, ("items", "seq"), scatter_dimension=0, tiled=True),
        lax.psum_scatter(flat_outer, ("items", "seq"), scatter_dimension=0, tiled=True),
        lax.psum_scatter(smalls, ("items", "seq"), scatter_dimension=0, tiled=True),
    )
    summed = (
        lax.all_gather(shares[0].astype(jnp.bfloat16), ("items", "seq"), axis=0, tiled=True).astype(
            jnp.float32
        ),
        lax.all_gather(shares[1].astype(jnp.bfloat16), ("items", "seq"), axis=0, tiled=True).astype(
            jnp.float32
        ),
        lax.all_gather(shares[2].astype(jnp.bfloat16), ("items", "seq"), axis=0, tiled=True).astype(
            jnp.float32
        ),
        lax.all_gather(shares[3].astype(jnp.bfloat16), ("items", "seq"), axis=0, tiled=True).astype(
            jnp.float32
        ),
        lax.all_gather(shares[4].astype(jnp.bfloat16), ("items", "seq"), axis=0, tiled=True).astype(
            jnp.float32
        ),
        lax.all_gather(shares[5].astype(jnp.bfloat16), ("items", "seq"), axis=0, tiled=True).astype(
            jnp.float32
        ),
        lax.all_gather(shares[6].astype(jnp.bfloat16), ("items", "seq"), axis=0, tiled=True).astype(
            jnp.float32
        ),
    )
    sum_query, sum_key, sum_value, sum_out, sum_inner, sum_outer, sum_small = summed
    width = D
    return (
        out_tokens,
        grad_tokens,
        sum_small[0:width],
        sum_small[width : 2 * width],
        sum_query.reshape(D, D),
        sum_small[2 * width : 3 * width],
        sum_key.reshape(D, D),
        sum_value.reshape(D, D),
        sum_small[3 * width : 4 * width],
        sum_out.reshape(D, D),
        sum_small[4 * width : 5 * width],
        sum_small[5 * width : 6 * width],
        sum_small[6 * width : 7 * width],
        sum_inner.reshape(D, FF),
        sum_small[8 * width : 8 * width + FF],
        sum_outer.reshape(FF, D),
        sum_small[7 * width : 8 * width],
    )


def solution(mesh):
    in_specs = (
        P("items", "seq", None),
        P("items", "seq", None),
        P(),
        P(),
        P(),
        P(),
        P(),
        P(),
        P(),
        P(),
        P(),
        P(),
        P(),
        P(),
        P(),
        P(),
        P(),
        P("items", None),
    )
    out_specs = (
        P("items", "seq", None),
        P("items", "seq", None),
        P(),
        P(),
        P(),
        P(),
        P(),
        P(),
        P(),
        P(),
        P(),
        P(),
        P(),
        P(),
        P(),
        P(),
        P(),
    )
    return jax.shard_map(local, mesh=mesh, in_specs=in_specs, out_specs=out_specs, check_vma=False)
```

profile of v0, /device:TPU:0, one launch (start us, length us, event | category | flops | bytes accessed | tf_op | source)
XLA Modules:
  0.0 1186.7 jit_solution(8166704738698876618)
XLA Ops:
  16.3 6.3 all-to-all-start
  25.9 16.9 %all-to-all-done = bf16[3,100,768]{1,0,2:T(4,128)(2,1)S(1)} async-done(((bf16[3,100,768]{1,0,2:T(4,128)(2,1)}), bf16[3,100,768]{1,0,2:T(4,128)(2,1)S(1)}, u32[]{:S(2)}, u32[]{:S(2)}) %all-to-all-start) | async-done | bytes 460832 | tf_op jit(solution)/shard_map/all_to_all | solution.py:99
  42.8 3.5 all-to-all-start.1
  46.3 2.6 convolution_convert_fusion.1
  50.7 2.2 copy.100
  52.9 13.0 %all-to-all-done.1 = bf16[3,100,768]{1,0,2:T(4,128)(2,1)S(1)} async-done(((bf16[3,100,768]{1,0,2:T(4,128)(2,1)}), bf16[3,100,768]{1,0,2:T(4,128)(2,1)S(1)}, u32[]{:S(2)}, u32[]{:S(2)}) %all-to-all-start.1) | async-done | bytes 460832 | tf_op jit(solution)/shard_map/all_to_all | solution.py:97
  65.9 4.2 all-to-all-start.2
  74.1 15.8 %all-to-all-done.2 = bf16[3,100,768]{1,0,2:T(4,128)(2,1)} async-done(((bf16[3,100,768]{1,0,2:T(4,128)(2,1)}), bf16[3,100,768]{1,0,2:T(4,128)(2,1)}, u32[]{:S(2)}, u32[]{:S(2)}) %all-to-all-start.2) | async-done | bytes 460832 | tf_op jit(solution)/shard_map/all_to_all | solution.py:98
  89.9 2.5 copy.102
  98.0 3.2 fusion.37
  101.2 2.3 copy.104
  103.5 3.7 all-to-all-start.3
  107.3 20.2 %all-to-all-done.3 = bf16[3,400,192]{2,0,1:T(4,128)(2,1)S(1)} async-done(((bf16[3,400,192]{2,0,1:T(4,128)(2,1)}), bf16[3,400,192]{2,0,1:T(4,128)(2,1)S(1)}, u32[]{:S(2)}, u32[]{:S(2)}) %all-to-all-start.3) | async-done | bytes 460832 | tf_op jit(solution)/shard_map/all_to_all | solution.py:112
  137.3 13.2 %negate_multiply_fusion = (f32[300,3072]{1,0:T(8,128)}, bf16[300,3072]{1,0:T(8,128)(2,1)}, f32[300,3072]{1,0:T(8,128)}) fusion(f32[3072]{0:T(1024)S(1)} %convert_element_type.162, bf16[300,768]{1,0:T(8,128)(2,1)} %reshape.289, bf16[768,3072]{1,0:T(8,128)(2,1)} %param.31), kind=kOutput, calls=%fused_computation.49 | convolution fusion | flops 1476403200 | bytes 14407680 | tf_op jit(solution)/shard_map/dot_general | solution.py:35
  150.5 3.8 mul.183
  154.3 3.8 mul.179
  158.1 13.9 %convert_reduce_fusion = (f32[3072]{0:T(1024)}, bf16[3,100,3072]{2,1,0:T(8,128)(2,1)S(1)}) fusion(f32[3,100,3072]{2,1,0:T(8,128)} %mul.183, f32[3,100,3072]{2,1,0:T(8,128)} %mul.179, bf16[3,100,768]{2,1,0:T(8,128)(2,1)} %param.19, bf16[3072,768]{1,0:T(8,128)(2,1)} %param.33), kind=kOutput, calls=%fused_computation.20 | convolution fusion | flops 1481008128 | bytes 14407680 | tf_op jit(solution)/shard_map/tj,ij->ti/dot_general | solution.py:39
  172.0 5.7 multiply_reduce_fusion.1
  180.1 2.8 convolution_convert_fusion
  185.2 4.7 all-to-all-start.4
  189.9 14.2 %convolution_bitcast_fusion = f32[3072,768]{1,0:T(8,128)} fusion(bf16[3,100,768]{2,1,0:T(8,128)(2,1)S(1)} %copy-done.24, f32[3,100,3072]{2,1,0:T(8,128)} %mul.179, f32[3,100,3072]{2,1,0:T(8,128)} %mul.183), kind=kOutput, calls=%fused_computation.8 | convolution fusion | flops 1472716800 | bytes 17270784 | tf_op jit(solution)/shard_map/ti,tj->ij/dot_general | solution.py:29
  204.7 3.2 fusion.78
  208.0 3.3 reshape.310
  211.3 2.5 copy.109
  215.4 5.5 multiply_reduce_fusion
  221.0 4.6 multiply_convert_fusion
  229.6 5.2 all-to-all-start.5
  234.8 4.4 convolution_bitcast_fusion.1
  239.2 5.9 copy.146
  245.1 10.8 reshape.316
  255.9 4.1 fusion.36
  260.0 2.2 copy.115
  262.2 5.1 all-to-all-start.6
  267.3 5.1 fusion.38
  276.9 2.2 fusion.75
  279.1 7.6 all-to-all-done.6
  286.7 3.5 all-to-all-start.7
  290.2 2.8 fusion.74
  293.0 2.3 copy.117
  297.4 2.2 fusion.76
  301.1 9.4 all-to-all-done.7
  313.6 2.2 fusion.77
  320.1 2.5 convert_reduce_fusion.2
  322.6 2.5 copy.139
  325.1 2.1 convert_reduce_fusion.4
  330.1 2.3 copy.143
  332.4 2.1 convert_reduce_fusion.3
  350.7 3.4 reshape.303
  354.0 3.2 reshape.306
  357.3 460.4 %all-reduce.10 = (bf16[9216]{0:T(1024)(128)(2,1)}, bf16[589824]{0:T(1024)(128)(2,1)}, bf16[589824]{0:T(1024)(128)(2,1)}, bf16[589824]{0:T(1024)(128)(2,1)}, bf16...) all-reduce(f32[9216]{0:T(1024)} %constant_dynamic-update-slice_fusi, ...), channel_id=2, replica_groups=mesh['items'=8,'seq'=4] {'items','seq'}, use_global_device_ids=true, to_apply=%region_20.21.clone | all-reduce | flops 7087104 | bytes 42522624
  826.9 2.8 dot_general.85
  829.7 5.4 fusion.47
  836.0 37.5 %all-reduce = bf16[9216]{0:T(1024)(128)(2,1)S(1)} all-reduce(bf16[9216]{0:T(1024)(128)(2,1)S(1)} %dynamic-update-slice), channel_id=1, replica_groups=mesh['items'=8,'seq'=4] {'items','seq'}, use_global_device_ids=true, to_apply=%add | all-reduce | flops 9216 | bytes 36864
  874.7 3.3 reshape.320
  878.1 49.6 %all-gather.9.cloned.1.call-done = bf16[589824]{0:T(1024)(128)(2,1)} async-done(((bf16[18432]{0:T(1024)(128)(2,1)}), bf16[589824]{0:T(1024)(128)(2,1)}) %all-gather.9.cloned.1.call-update) | async-done | bytes 1179664 | tf_op jit(solution)/shard_map/all_gather | solution.py:215
  927.7 3.3 reshape.322
  931.0 52.4 %all-gather.11.cloned.1.call-done = bf16[589824]{0:T(1024)(128)(2,1)} async-done(((bf16[18432]{0:T(1024)(128)(2,1)}), bf16[589824]{0:T(1024)(128)(2,1)}) %all-gather.11.cloned.1.call-update) | async-done | bytes 1179664 | tf_op jit(solution)/shard_map/all_gather | solution.py:218
  983.5 3.3 reshape.324
  986.8 52.3 %all-gather.13.cloned.1.call-done = bf16[589824]{0:T(1024)(128)(2,1)} async-done(((bf16[18432]{0:T(1024)(128)(2,1)}), bf16[589824]{0:T(1024)(128)(2,1)}) %all-gather.13.cloned.1.call-update) | async-done | bytes 1179664 | tf_op jit(solution)/shard_map/all_gather | solution.py:221
  1039.1 3.3 reshape.326
  1042.4 62.4 %all-gather.15.cloned.1.call-done = bf16[2359296]{0:T(1024)(128)(2,1)} async-done(((bf16[73728]{0:T(1024)(128)(2,1)}), bf16[2359296]{0:T(1024)(128)(2,1)}) %all-gather.15.cloned.1.call-update) | async-done | bytes 4718608 | tf_op jit(solution)/shard_map/all_gather | solution.py:224
  1104.8 8.7 reshape.328
  1113.6 55.8 %all-gather.17.cloned.1.call-done = bf16[2359296]{0:T(1024)(128)(2,1)} async-done(((bf16[73728]{0:T(1024)(128)(2,1)}), bf16[2359296]{0:T(1024)(128)(2,1)}) %all-gather.17.cloned.1.call-update) | async-done | bytes 4718608 | tf_op jit(solution)/shard_map/all_gather | solution.py:227
  1169.4 10.0 reshape.330
  (196 shorter events, 90.0 us)
Async XLA Ops:
  7.2 7.2 copy-start
  8.7 3.1 copy-start.30
  9.9 1.9 copy-start.32
  11.2 0.6 copy-start.36
  11.8 0.6 copy-start.34
  13.6 9.1 copy-start.41
  13.7 32.6 %copy-start.9 = (bf16[300,768]{1,0:T(8,128)(2,1)}, bf16[300,768]{1,0:T(8,128)(2,1)S(1)}, u32[]{:S(2)}) copy-start(bf16[300,768]{1,0:T(8,128)(2,1)S(1)} %reshape.281) | copy-start | bytes 1382404
  16.3 26.5 %all-to-all-start = ((bf16[3,100,768]{1,0,2:T(4,128)(2,1)}), bf16[3,100,768]{1,0,2:T(4,128)(2,1)S(1)}, u32[]{:S(2)}, u32[]{:S(2)}) async-start(bf16[3,100,768]{1,0,2:T(4,128)(2,1)} %copy.94), calls=%async_computation | async-start | bytes 1572864 | tf_op jit(solution)/shard_map/all_to_all | solution.py:99
  25.9 44.3 %copy-start.39 = (s32[3,400]{1,0:T(4,128)S(1)}, s32[3,400]{1,0:T(4,128)}, u32[]{:S(2)}) copy-start(s32[3,400]{1,0:T(4,128)} %param.35) | copy-start | bytes 14404
  42.8 23.1 %all-to-all-start.1 = ((bf16[3,100,768]{1,0,2:T(4,128)(2,1)}), bf16[3,100,768]{1,0,2:T(4,128)(2,1)S(1)}, u32[]{:S(2)}, u32[]{:S(2)}) async-start(bf16[3,100,768]{1,0,2:T(4,128)(2,1)} %copy.97), calls=%async_computation.1 | async-start | bytes 1572864 | tf_op jit(solution)/shard_map/all_to_all | solution.py:97
  65.9 23.9 %all-to-all-start.2 = ((bf16[3,100,768]{1,0,2:T(4,128)(2,1)}), bf16[3,100,768]{1,0,2:T(4,128)(2,1)}, u32[]{:S(2)}, u32[]{:S(2)}) async-start(bf16[3,100,768]{1,0,2:T(4,128)(2,1)} %copy.100), calls=%async_computation.2 | async-start | bytes 1572864 | tf_op jit(solution)/shard_map/all_to_all | solution.py:98
  73.2 24.8 %copy-start.20 = (bf16[3,400,3,64]{1,3,2,0:T(8,128)(2,1)}, bf16[3,400,3,64]{1,3,2,0:T(8,128)(2,1)S(1)}, u32[]{:S(2)}) copy-start(bf16[3,400,3,64]{1,3,2,0:T(8,128)(2,1)S(1)} %reshape.283) | copy-start | bytes 1382404
  94.0 1.9 copy-start.13
  95.9 5.2 copy-start.1
  98.0 9.2 copy-start.42
  98.0 9.3 copy-start.40
  98.0 9.3 copy-start.43
  98.0 9.3 copy-start.44
  101.2 30.9 %copy-start.3 = (bf16[3,100,768]{2,1,0:T(8,128)(2,1)S(1)}, bf16[3,100,768]{2,1,0:T(8,128)(2,1)}, u32[]{:S(2)}) copy-start(bf16[3,100,768]{2,1,0:T(8,128)(2,1)} %param.18) | copy-start | bytes 1382404
  103.5 24.0 %all-to-all-start.3 = ((bf16[3,400,192]{2,0,1:T(4,128)(2,1)}), bf16[3,400,192]{2,0,1:T(4,128)(2,1)S(1)}, u32[]{:S(2)}, u32[]{:S(2)}) async-start(bf16[3,400,192]{2,0,1:T(4,128)(2,1)} %copy.104), calls=%async_computation.3 | async-start | bytes 1638400 | tf_op jit(solution)/shard_map/all_to_all | solution.py:112
  107.3 113.7 %copy-start.28 = (f32[3,3,400]{2,1,0:T(4,128)}, f32[3,3,400]{2,1,0:T(4,128)S(1)}, u32[]{:S(2)}) copy-start(f32[3,3,400]{2,1,0:T(4,128)S(1)} %log_add_fusion) | copy-start | bytes 43204
  127.5 0.9 copy-start.19
  129.9 0.8 copy-start.15
  134.2 43.5 %copy-start.7 = (f32[3,100,768]{2,1,0:T(8,128)}, f32[3,100,768]{2,1,0:T(8,128)S(1)}, u32[]{:S(2)}) copy-start(f32[3,100,768]{2,1,0:T(8,128)S(1)} %get-tuple-element.48) | copy-start | bytes 2764804
  172.0 5.7 copy-start.26
  172.0 7.0 copy-start.23
  178.1 0.9 copy-start.6
  179.3 10.7 copy-start.24
  185.2 26.1 %all-to-all-start.4 = ((bf16[3,100,768]{1,0,2:T(4,128)(2,1)}), bf16[3,100,768]{1,0,2:T(4,128)(2,1)}, u32[]{:S(2)}, u32[]{:S(2)}) async-start(bf16[3,100,768]{1,0,2:T(4,128)(2,1)} %copy.107), calls=%async_computation.4 | async-start | bytes 1572864 | tf_op jit(solution)/shard_map/all_to_all | solution.py:141
  189.9 14.3 %copy-start.16 = (bf16[3,100,4,192]{3,2,1,0:T(4,128)(2,1)S(1)}, bf16[3,100,4,192]{3,2,1,0:T(4,128)(2,1)}, u32[]{:S(2)}) copy-start(bf16[3,100,4,192]{3,2,1,0:T(4,128)(2,1)} %copy-done.15) | copy-start | bytes 1382404
  208.0 7.4 copy-start.21
  215.4 5.6 copy-start.22
  221.0 6.4 copy-start.14
  225.6 1.8 copy-start.2
  229.6 32.6 %all-to-all-start.5 = ((bf16[3,400,192]{2,0,1:T(4,128)(2,1)}), bf16[3,400,192]{2,0,1:T(4,128)(2,1)S(1)}, u32[]{:S(2)}, u32[]{:S(2)}) async-start(bf16[3,400,192]{2,0,1:T(4,128)(2,1)} %copy.111), calls=%async_computation.5 | async-start | bytes 1638400 | tf_op jit(solution)/shard_map/all_to_all | solution.py:169
  255.9 11.4 copy-start.29
  262.2 11.6 copy-start.11
  262.2 24.5 %all-to-all-start.6 = ((bf16[3,400,192]{2,0,1:T(4,128)(2,1)}), bf16[3,400,192]{2,0,1:T(4,128)(2,1)}, u32[]{:S(2)}, u32[]{:S(2)}) async-start(bf16[3,400,192]{2,0,1:T(4,128)(2,1)} %copy.115), calls=%async_computation.6 | async-start | bytes 1638400 | tf_op jit(solution)/shard_map/all_to_all | solution.py:170
  272.4 4.5 copy-start.10
  286.7 23.8 %all-to-all-start.7 = ((bf16[3,400,192]{2,0,1:T(4,128)(2,1)}), bf16[3,400,192]{2,0,1:T(4,128)(2,1)S(1)}, u32[]{:S(2)}, u32[]{:S(2)}) async-start(bf16[3,400,192]{2,0,1:T(4,128)(2,1)} %copy.119), calls=%async_computation.7 | async-start | bytes 1638400 | tf_op jit(solution)/shard_map/all_to_all | solution.py:171
  290.2 584.5 %all-gather.7.cloned.1.call-start = ((), (), s32[]{:S(2)}) async-start(), calls=%async_computation.8 | async-start | bytes 1216512 | tf_op jit(solution)/shard_map/all_gather | solution.py:212
  297.4 2.2 copy-start.17
  297.4 2.2 copy-start.27
  310.5 6.8 copy-start.12
  313.6 2.2 copy-start.18
  313.6 5.1 copy-start.31
  313.6 5.1 copy-start.33
  315.8 3.2 copy-start.37
  315.8 3.2 copy-start.35
  317.3 2.8 copy-start.25
  322.6 14.8 %copy-start.38 = (f32[768]{0:T(1024)S(1)}, f32[768]{0:T(1024)}, u32[]{:S(2)}) copy-start(f32[768]{0:T(1024)} %get-tuple-element.19) | copy-start | bytes 9220
  322.6 26.5 %copy-start.5 = (f32[768,768]{1,0:T(8,128)S(1)}, f32[768,768]{1,0:T(8,128)}, u32[]{:S(2)}) copy-start(f32[768,768]{1,0:T(8,128)} %fusion.75) | copy-start | bytes 7077892
  350.7 6.6 copy-start.4
  357.3 469.6 %copy-start.45 = (bf16[768]{0:T(1024)(128)(2,1)S(1)}, bf16[768]{0:T(1024)(128)(2,1)}, u32[]{:S(2)}) copy-start(bf16[768]{0:T(1024)(128)(2,1)} %param.34) | copy-start | bytes 4612
  817.7 12.0 %copy-start.8 = (f32[3,100,768]{2,1,0:T(8,128)S(1)}, f32[3,100,768]{2,1,0:T(8,128)}, u32[]{:S(2)}) copy-start(f32[3,100,768]{2,1,0:T(8,128)} %copy-done.7) | copy-start | bytes 2764804
  819.2 108.5 %all-gather.9.cloned.1.call-start = ((), (), s32[]{:S(2)}) async-start(), calls=%async_computation.9 | async-start | bytes 1216512 | tf_op jit(solution)/shard_map/all_gather | solution.py:215
  820.6 162.8 %all-gather.11.cloned.1.call-start = ((), (), s32[]{:S(2)}) async-start(), calls=%async_computation.10 | async-start | bytes 1216512 | tf_op jit(solution)/shard_map/all_gather | solution.py:218
  822.1 216.9 %all-gather.13.cloned.1.call-start = ((), (), s32[]{:S(2)}) async-start(), calls=%async_computation.11 | async-start | bytes 1216512 | tf_op jit(solution)/shard_map/all_gather | solution.py:221
  823.6 281.3 %all-gather.15.cloned.1.call-start = ((), (), s32[]{:S(2)}) async-start(), calls=%async_computation.12 | async-start | bytes 4866048 | tf_op jit(solution)/shard_map/all_gather | solution.py:224
  825.2 344.2 %all-gather.17.cloned.1.call-start = ((), (), s32[]{:S(2)}) async-start(), calls=%async_computation.13 | async-start | bytes 4866048 | tf_op jit(solution)/shard_map/all_gather | solution.py:227
Sparse Core Ops, SparseCore 0:
  819.3 52.1 all-gather.6
  874.9 52.7 all-gather.8
  930.5 52.9 all-gather.10
  986.1 52.8 all-gather.12
  1042.3 62.5 all-gather.14
  1107.5 61.8 all-gather.16
where the time goes:
time: 1200 us; the launch traced here: 1190 us
  blocking collectives  498 us (42%)
  waiting for transfers between devices  356 us (30%)
  local copies, waits for them, and re-layouts  156 us (13%)
  matrix products  103 us (9%)
  starting transfers between devices  36.5 us (3%)
  other arithmetic  22.6 us (2%)
  between operations  15.3 us (1%)
    unnamed x2, blocking collectives  498 us
    all_gather x1, waiting for transfers between devices, local(): lax.all_gather(shares[4].astype(jnp.bfloat16), ('items', 'seq'), axis=0,...  62.4 us
    all_gather x1, waiting for transfers between devices, local(): lax.all_gather(shares[5].astype(jnp.bfloat16), ('items', 'seq'), axis=0,...  55.8 us
    all_gather x1, waiting for transfers between devices, local(): lax.all_gather(shares[2].astype(jnp.bfloat16), ('items', 'seq'), axis=0,...  52.4 us
    all_gather x1, waiting for transfers between devices, local(): lax.all_gather(shares[3].astype(jnp.bfloat16), ('items', 'seq'), axis=0,...  52.3 us
    all_gather x1, waiting for transfers between devices, local(): lax.all_gather(shares[1].astype(jnp.bfloat16), ('items', 'seq'), axis=0,...  49.6 us
    unnamed x110, local copies, waits for them, and re-layouts  31.7 us
    dot_general x6, matrix products, tall_dot(): jnp.einsum('ti,tj->ij', flat_rows(left), flat_rows(right), preferred_elem...  28.5 us
  transfers between devices with their start and end apart: 14, of which 11 were waited for; matrix products, arithmetic and copies ran while one was open for 11% of the time, Pallas kernels for 0%

commit v1 on v0

--- a/solution.py
+++ b/solution.py
@@ -9,6 +9,27 @@
 FF = 3072
 EPSILON = 1e-06
 MASKED = -1000000000.0
+
+
+def laid_out(blocks, dim):
+    shape = list(blocks.shape[1:])
+    shape[dim] *= blocks.shape[0]
+    return jnp.moveaxis(blocks, 0, dim).reshape(shape)
+
+
+def doubled(value, axis):
+    size, index = (lax.axis_size(axis), lax.axis_index(axis))
+    parts, distance = (value[None], 1)
+    while distance < size:
+        other = lax.ppermute(parts, axis, [(i, i ^ distance) for i in range(size)])
+        low = index & distance == 0
+        parts = jnp.concatenate([jnp.where(low, parts, other), jnp.where(low, other, parts)])
+        distance *= 2
+    return parts
+
+
+def collect(value, axis, dim):
+    return laid_out(doubled(value, axis), dim)
 
 
 def norm_rows(values, gain, shift):
@@ -218,9 +239,7 @@
         lax.all_gather(shares[2].astype(jnp.bfloat16), ("items", "seq"), axis=0, tiled=True).astype(
             jnp.float32
         ),
-        lax.all_gather(shares[3].astype(jnp.bfloat16), ("items", "seq"), axis=0, tiled=True).astype(
-            jnp.float32
-        ),
+        collect(shares[3].astype(jnp.bfloat16), ("items", "seq"), 0).astype(jnp.float32),
         lax.all_gather(shares[4].astype(jnp.bfloat16), ("items", "seq"), axis=0, tiled=True).astype(
             jnp.float32
         ),

time: 1200 us -> 1140 us (0.950)
  waiting for transfers between devices: 356 us -> 292 us
    all_gather x1 -> x0, waiting for transfers between devices: 52.3 us -> none  [local(): lax.all_gather(shares[3].astype(jnp.bfloat16), ('items', 'seq'), axis=0,...]
    all_gather x1, waiting for transfers between devices: 49.6 us -> 26.8 us  [local(): lax.all_gather(shares[1].astype(jnp.bfloat16), ('items', 'seq'), axis=0,...]
  transfers between devices with their start and end apart: 14 -> 18, of which waited for: 11 -> 14; matrix products, arithmetic and copies ran while one was open for 11% -> 11% of each run, Pallas kernels for 0% -> 0%
where the time goes in v1:
time: 1140 us; the launch traced here: 1130 us
  blocking collectives  502 us (44%)
  waiting for transfers between devices  292 us (26%)
  local copies, waits for them, and re-layouts  154 us (14%)
  matrix products  103 us (9%)
  starting transfers between devices  40.1 us (4%)
  other arithmetic  25.1 us (2%)
  between operations  15.1 us (1%)
    unnamed x2, blocking collectives  502 us
    all_gather x1, waiting for transfers between devices, local(): lax.all_gather(shares[4].astype(jnp.bfloat16), ('items', 'seq'), axis=0,...  62.4 us
    all_gather x1, waiting for transfers between devices, local(): lax.all_gather(shares[5].astype(jnp.bfloat16), ('items', 'seq'), axis=0,...  55.8 us
    all_gather x1, waiting for transfers between devices, local(): lax.all_gather(shares[2].astype(jnp.bfloat16), ('items', 'seq'), axis=0,...  52.4 us
    unnamed x110, local copies, waits for them, and re-layouts  31.1 us
    dot_general x6, matrix products, tall_dot(): jnp.einsum('ti,tj->ij', flat_rows(left), flat_rows(right), preferred_elem...  28.5 us
    dot_general x6, matrix products, back_dot(): jnp.einsum('tj,ij->ti', flat_rows(grads), weight, preferred_element_type=...  28.1 us
    all_gather x1, waiting for transfers between devices, local(): lax.all_gather(shares[1].astype(jnp.bfloat16), ('items', 'seq'), axis=0,...  26.8 us
  transfers between devices with their start and end apart: 18, of which 14 were waited for; matrix products, arithmetic and copies ran while one was open for 11% of the time, Pallas kernels for 0%

profile of v1, /device:TPU:0, one launch (start us, length us, event | category | flops | bytes accessed | tf_op | source)
XLA Modules:
  0.0 1130.3 jit_solution(2910784164387810673)
XLA Ops:
  16.3 6.3 all-to-all-start
  25.9 16.9 %all-to-all-done = bf16[3,100,768]{1,0,2:T(4,128)(2,1)S(1)} async-done(((bf16[3,100,768]{1,0,2:T(4,128)(2,1)}), bf16[3,100,768]{1,0,2:T(4,128)(2,1)S(1)}, u32[]{:S(2)}, u32[]{:S(2)}) %all-to-all-start) | async-done | bytes 460832 | tf_op jit(solution)/shard_map/all_to_all | solution.py:120
  42.8 3.5 all-to-all-start.1
  46.3 2.6 convolution_convert_fusion.1
  50.7 2.2 copy.100
  52.9 13.0 %all-to-all-done.1 = bf16[3,100,768]{1,0,2:T(4,128)(2,1)S(1)} async-done(((bf16[3,100,768]{1,0,2:T(4,128)(2,1)}), bf16[3,100,768]{1,0,2:T(4,128)(2,1)S(1)}, u32[]{:S(2)}, u32[]{:S(2)}) %all-to-all-start.1) | async-done | bytes 460832 | tf_op jit(solution)/shard_map/all_to_all | solution.py:118
  65.9 4.2 all-to-all-start.2
  74.1 15.8 %all-to-all-done.2 = bf16[3,100,768]{1,0,2:T(4,128)(2,1)} async-done(((bf16[3,100,768]{1,0,2:T(4,128)(2,1)}), bf16[3,100,768]{1,0,2:T(4,128)(2,1)}, u32[]{:S(2)}, u32[]{:S(2)}) %all-to-all-start.2) | async-done | bytes 460832 | tf_op jit(solution)/shard_map/all_to_all | solution.py:119
  89.8 2.5 copy.102
  98.0 3.2 fusion.37
  101.2 2.3 copy.104
  103.5 3.7 all-to-all-start.3
  107.3 20.2 %all-to-all-done.3 = bf16[3,400,192]{2,0,1:T(4,128)(2,1)S(1)} async-done(((bf16[3,400,192]{2,0,1:T(4,128)(2,1)}), bf16[3,400,192]{2,0,1:T(4,128)(2,1)S(1)}, u32[]{:S(2)}, u32[]{:S(2)}) %all-to-all-start.3) | async-done | bytes 460832 | tf_op jit(solution)/shard_map/all_to_all | solution.py:133
  137.3 13.2 %negate_multiply_fusion = (f32[300,3072]{1,0:T(8,128)}, bf16[300,3072]{1,0:T(8,128)(2,1)}, f32[300,3072]{1,0:T(8,128)}) fusion(f32[3072]{0:T(1024)S(1)} %convert_element_type.168, bf16[300,768]{1,0:T(8,128)(2,1)} %reshape.288, bf16[768,3072]{1,0:T(8,128)(2,1)} %param.31), kind=kOutput, calls=%fused_computation.49 | convolution fusion | flops 1476403200 | bytes 14407680 | tf_op jit(solution)/shard_map/dot_general | solution.py:56
  150.5 3.8 mul.186
  154.3 3.8 mul.182
  158.1 13.9 %convert_reduce_fusion = (f32[3072]{0:T(1024)}, bf16[3,100,3072]{2,1,0:T(8,128)(2,1)S(1)}) fusion(f32[3,100,3072]{2,1,0:T(8,128)} %mul.186, f32[3,100,3072]{2,1,0:T(8,128)} %mul.182, bf16[3,100,768]{2,1,0:T(8,128)(2,1)} %param.19, bf16[3072,768]{1,0:T(8,128)(2,1)} %param.33), kind=kOutput, calls=%fused_computation.20 | convolution fusion | flops 1481008128 | bytes 14407680 | tf_op jit(solution)/shard_map/tj,ij->ti/dot_general | solution.py:60
  172.1 5.7 multiply_reduce_fusion.1
  180.1 2.8 convolution_convert_fusion
  185.3 4.7 all-to-all-start.4
  189.9 14.2 %convolution_bitcast_fusion = f32[3072,768]{1,0:T(8,128)} fusion(bf16[3,100,768]{2,1,0:T(8,128)(2,1)S(1)} %copy-done.24, f32[3,100,3072]{2,1,0:T(8,128)} %mul.182, f32[3,100,3072]{2,1,0:T(8,128)} %mul.186), kind=kOutput, calls=%fused_computation.8 | convolution fusion | flops 1472716800 | bytes 17270784 | tf_op jit(solution)/shard_map/ti,tj->ij/dot_general | solution.py:50
  204.8 3.2 fusion.78
  208.0 3.3 reshape.309
  211.3 2.5 copy.109
  215.4 5.5 multiply_reduce_fusion
  221.0 4.6 multiply_convert_fusion
  229.6 5.2 all-to-all-start.5
  234.8 4.4 convolution_bitcast_fusion.1
  239.2 5.9 copy.146
  245.1 10.8 reshape.313
  255.9 4.1 fusion.36
  259.9 2.2 copy.115
  262.2 5.1 all-to-all-start.6
  267.3 5.1 fusion.38
  276.8 2.2 fusion.75
  279.1 7.6 all-to-all-done.6
  286.6 3.5 all-to-all-start.7
  290.2 2.8 fusion.74
  293.0 2.3 copy.117
  297.4 2.2 fusion.76
  301.1 9.4 all-to-all-done.7
  313.5 2.2 fusion.77
  320.1 2.5 convert_reduce_fusion.2
  322.6 2.5 copy.139
  330.1 2.3 copy.143
  332.4 2.1 convert_reduce_fusion.3
  350.6 3.4 reshape.302
  354.0 3.2 reshape.305
  357.2 460.4 %all-reduce.10 = (bf16[9216]{0:T(1024)(128)(2,1)}, bf16[589824]{0:T(1024)(128)(2,1)}, bf16[589824]{0:T(1024)(128)(2,1)}, bf16[589824]{0:T(1024)(128)(2,1)}, bf16...) all-reduce(f32[9216]{0:T(1024)} %constant_dynamic-update-slice_fusi, ...), channel_id=2, replica_groups=mesh['items'=8,'seq'=4] {'items','seq'}, use_global_device_ids=true, to_apply=%region_20.21.clone | all-reduce | flops 7087104 | bytes 42522624
  823.0 2.9 collective-permute-done
  827.9 4.0 collective-permute-done.1
  835.7 2.8 dot_general.85
  840.1 3.1 collective-permute-done.3
  846.1 5.4 fusion.47
  852.5 41.4 %all-reduce = bf16[9216]{0:T(1024)(128)(2,1)S(1)} all-reduce(bf16[9216]{0:T(1024)(128)(2,1)S(1)} %dynamic-update-slice), channel_id=1, replica_groups=mesh['items'=8,'seq'=4] {'items','seq'}, use_global_device_ids=true, to_apply=%add | all-reduce | flops 9216 | bytes 36864
  897.0 3.3 reshape.317
  900.4 26.8 %all-gather.8.cloned.1.call-done = bf16[589824]{0:T(1024)(128)(2,1)} async-done(((bf16[18432]{0:T(1024)(128)(2,1)}), bf16[589824]{0:T(1024)(128)(2,1)}) %all-gather.8.cloned.1.call-update) | async-done | bytes 1179664 | tf_op jit(solution)/shard_map/all_gather | solution.py:236
  927.2 3.3 reshape.319
  930.6 52.4 %all-gather.10.cloned.1.call-done = bf16[589824]{0:T(1024)(128)(2,1)} async-done(((bf16[18432]{0:T(1024)(128)(2,1)}), bf16[589824]{0:T(1024)(128)(2,1)}) %all-gather.10.cloned.1.call-update) | async-done | bytes 1179664 | tf_op jit(solution)/shard_map/all_gather | solution.py:239
  983.0 3.3 reshape.321
  986.3 62.4 %all-gather.12.cloned.1.call-done = bf16[2359296]{0:T(1024)(128)(2,1)} async-done(((bf16[73728]{0:T(1024)(128)(2,1)}), bf16[2359296]{0:T(1024)(128)(2,1)}) %all-gather.12.cloned.1.call-update) | async-done | bytes 4718608 | tf_op jit(solution)/shard_map/all_gather | solution.py:243
  1048.8 8.7 reshape.324
  1057.5 55.8 %all-gather.14.cloned.1.call-done = bf16[2359296]{0:T(1024)(128)(2,1)} async-done(((bf16[73728]{0:T(1024)(128)(2,1)}), bf16[2359296]{0:T(1024)(128)(2,1)}) %all-gather.14.cloned.1.call-update) | async-done | bytes 4718608 | tf_op jit(solution)/shard_map/all_gather | solution.py:246
  1113.3 10.0 reshape.326
  (214 shorter events, 100.5 us)
Async XLA Ops:
  7.2 7.2 copy-start
  8.7 3.1 copy-start.30
  9.9 1.9 copy-start.32
  11.2 0.6 copy-start.36
  11.8 0.6 copy-start.34
  13.6 9.1 copy-start.41
  13.7 32.6 %copy-start.9 = (bf16[300,768]{1,0:T(8,128)(2,1)}, bf16[300,768]{1,0:T(8,128)(2,1)S(1)}, u32[]{:S(2)}) copy-start(bf16[300,768]{1,0:T(8,128)(2,1)S(1)} %reshape.280) | copy-start | bytes 1382404
  16.3 26.5 %all-to-all-start = ((bf16[3,100,768]{1,0,2:T(4,128)(2,1)}), bf16[3,100,768]{1,0,2:T(4,128)(2,1)S(1)}, u32[]{:S(2)}, u32[]{:S(2)}) async-start(bf16[3,100,768]{1,0,2:T(4,128)(2,1)} %copy.94), calls=%async_computation | async-start | bytes 1572864 | tf_op jit(solution)/shard_map/all_to_all | solution.py:120
  25.9 44.3 %copy-start.39 = (s32[3,400]{1,0:T(4,128)S(1)}, s32[3,400]{1,0:T(4,128)}, u32[]{:S(2)}) copy-start(s32[3,400]{1,0:T(4,128)} %param.35) | copy-start | bytes 14404
  42.8 23.1 %all-to-all-start.1 = ((bf16[3,100,768]{1,0,2:T(4,128)(2,1)}), bf16[3,100,768]{1,0,2:T(4,128)(2,1)S(1)}, u32[]{:S(2)}, u32[]{:S(2)}) async-start(bf16[3,100,768]{1,0,2:T(4,128)(2,1)} %copy.97), calls=%async_computation.1 | async-start | bytes 1572864 | tf_op jit(solution)/shard_map/all_to_all | solution.py:118
  65.9 23.9 %all-to-all-start.2 = ((bf16[3,100,768]{1,0,2:T(4,128)(2,1)}), bf16[3,100,768]{1,0,2:T(4,128)(2,1)}, u32[]{:S(2)}, u32[]{:S(2)}) async-start(bf16[3,100,768]{1,0,2:T(4,128)(2,1)} %copy.100), calls=%async_computation.2 | async-start | bytes 1572864 | tf_op jit(solution)/shard_map/all_to_all | solution.py:119
  73.1 24.8 %copy-start.20 = (bf16[3,400,3,64]{1,3,2,0:T(8,128)(2,1)}, bf16[3,400,3,64]{1,3,2,0:T(8,128)(2,1)S(1)}, u32[]{:S(2)}) copy-start(bf16[3,400,3,64]{1,3,2,0:T(8,128)(2,1)S(1)} %reshape.282) | copy-start | bytes 1382404
  94.0 1.9 copy-start.13
  95.9 5.2 copy-start.1
  98.0 9.2 copy-start.42
  98.0 9.3 copy-start.40
  98.0 9.3 copy-start.43
  98.0 9.3 copy-start.44
  101.2 30.9 %copy-start.3 = (bf16[3,100,768]{2,1,0:T(8,128)(2,1)S(1)}, bf16[3,100,768]{2,1,0:T(8,128)(2,1)}, u32[]{:S(2)}) copy-start(bf16[3,100,768]{2,1,0:T(8,128)(2,1)} %param.18) | copy-start | bytes 1382404
  103.5 24.0 %all-to-all-start.3 = ((bf16[3,400,192]{2,0,1:T(4,128)(2,1)}), bf16[3,400,192]{2,0,1:T(4,128)(2,1)S(1)}, u32[]{:S(2)}, u32[]{:S(2)}) async-start(bf16[3,400,192]{2,0,1:T(4,128)(2,1)} %copy.104), calls=%async_computation.3 | async-start | bytes 1638400 | tf_op jit(solution)/shard_map/all_to_all | solution.py:133
  107.3 113.7 %copy-start.28 = (f32[3,3,400]{2,1,0:T(4,128)}, f32[3,3,400]{2,1,0:T(4,128)S(1)}, u32[]{:S(2)}) copy-start(f32[3,3,400]{2,1,0:T(4,128)S(1)} %log_add_fusion) | copy-start | bytes 43204
  127.5 0.9 copy-start.19
  129.9 0.8 copy-start.15
  134.2 43.6 %copy-start.7 = (f32[3,100,768]{2,1,0:T(8,128)}, f32[3,100,768]{2,1,0:T(8,128)S(1)}, u32[]{:S(2)}) copy-start(f32[3,100,768]{2,1,0:T(8,128)S(1)} %get-tuple-element.58) | copy-start | bytes 2764804
  172.1 5.7 copy-start.26
  172.1 7.0 copy-start.23
  178.2 0.9 copy-start.6
  179.3 10.6 copy-start.24
  185.3 26.0 %all-to-all-start.4 = ((bf16[3,100,768]{1,0,2:T(4,128)(2,1)}), bf16[3,100,768]{1,0,2:T(4,128)(2,1)}, u32[]{:S(2)}, u32[]{:S(2)}) async-start(bf16[3,100,768]{1,0,2:T(4,128)(2,1)} %copy.107), calls=%async_computation.4 | async-start | bytes 1572864 | tf_op jit(solution)/shard_map/all_to_all | solution.py:162
  189.9 14.3 %copy-start.16 = (bf16[3,100,4,192]{3,2,1,0:T(4,128)(2,1)S(1)}, bf16[3,100,4,192]{3,2,1,0:T(4,128)(2,1)}, u32[]{:S(2)}) copy-start(bf16[3,100,4,192]{3,2,1,0:T(4,128)(2,1)} %copy-done.15) | copy-start | bytes 1382404
  208.0 7.4 copy-start.21
  215.4 5.6 copy-start.22
  221.0 6.4 copy-start.14
  225.6 1.8 copy-start.2
  229.6 32.6 %all-to-all-start.5 = ((bf16[3,400,192]{2,0,1:T(4,128)(2,1)}), bf16[3,400,192]{2,0,1:T(4,128)(2,1)S(1)}, u32[]{:S(2)}, u32[]{:S(2)}) async-start(bf16[3,400,192]{2,0,1:T(4,128)(2,1)} %copy.111), calls=%async_computation.5 | async-start | bytes 1638400 | tf_op jit(solution)/shard_map/all_to_all | solution.py:190
  255.9 11.4 %copy-start.29 = (f32[3,3,400]{2,1,0:T(4,128)S(1)}, f32[3,3,400]{2,1,0:T(4,128)}, u32[]{:S(2)}) copy-start(f32[3,3,400]{2,1,0:T(4,128)} %copy-done.28) | copy-start | bytes 43204
  262.2 11.6 %copy-start.11 = (bf16[3,400,192]{2,0,1:T(4,128)(2,1)}, bf16[3,400,192]{2,0,1:T(4,128)(2,1)S(1)}, u32[]{:S(2)}) copy-start(bf16[3,400,192]{2,0,1:T(4,128)(2,1)S(1)} %all-to-all-done.5) | copy-start | bytes 1382404
  262.2 24.5 %all-to-all-start.6 = ((bf16[3,400,192]{2,0,1:T(4,128)(2,1)}), bf16[3,400,192]{2,0,1:T(4,128)(2,1)}, u32[]{:S(2)}, u32[]{:S(2)}) async-start(bf16[3,400,192]{2,0,1:T(4,128)(2,1)} %copy.115), calls=%async_computation.6 | async-start | bytes 1638400 | tf_op jit(solution)/shard_map/all_to_all | solution.py:191
  272.4 4.5 copy-start.10
  286.6 23.8 %all-to-all-start.7 = ((bf16[3,400,192]{2,0,1:T(4,128)(2,1)}), bf16[3,400,192]{2,0,1:T(4,128)(2,1)S(1)}, u32[]{:S(2)}, u32[]{:S(2)}) async-start(bf16[3,400,192]{2,0,1:T(4,128)(2,1)} %copy.119), calls=%async_computation.7 | async-start | bytes 1638400 | tf_op jit(solution)/shard_map/all_to_all | solution.py:192
  290.1 606.9 %all-gather.6.cloned.1.call-start = ((), (), s32[]{:S(2)}) async-start(), calls=%async_computation.8 | async-start | bytes 1216512 | tf_op jit(solution)/shard_map/all_gather | solution.py:233
  297.3 2.2 copy-start.17
  297.3 2.2 copy-start.27
  310.5 6.8 copy-start.12
  313.5 2.2 copy-start.18
  313.5 5.1 copy-start.31
  313.5 5.1 copy-start.33
  315.8 3.2 copy-start.37
  315.8 3.2 copy-start.35
  317.3 2.8 copy-start.25
  322.6 14.8 %copy-start.38 = (f32[768]{0:T(1024)S(1)}, f32[768]{0:T(1024)}, u32[]{:S(2)}) copy-start(f32[768]{0:T(1024)} %get-tuple-element.19) | copy-start | bytes 9220
  322.6 26.5 %copy-start.5 = (f32[768,768]{1,0:T(8,128)S(1)}, f32[768,768]{1,0:T(8,128)}, u32[]{:S(2)}) copy-start(f32[768,768]{1,0:T(8,128)} %fusion.75) | copy-start | bytes 7077892
  350.6 6.6 copy-start.4
  357.2 478.5 %copy-start.45 = (bf16[768]{0:T(1024)(128)(2,1)S(1)}, bf16[768]{0:T(1024)(128)(2,1)}, u32[]{:S(2)}) copy-start(bf16[768]{0:T(1024)(128)(2,1)} %param.34) | copy-start | bytes 4612
  819.1 108.1 %all-gather.8.cloned.1.call-start = ((), (), s32[]{:S(2)}) async-start(), calls=%async_computation.9 | async-start | bytes 1216512 | tf_op jit(solution)/shard_map/all_gather | solution.py:236
  820.5 162.4 %all-gather.10.cloned.1.call-start = ((), (), s32[]{:S(2)}) async-start(), calls=%async_computation.10 | async-start | bytes 1216512 | tf_op jit(solution)/shard_map/all_gather | solution.py:239
  821.4 4.4 collective-permute-start
  822.9 225.9 %all-gather.12.cloned.1.call-start = ((), (), s32[]{:S(2)}) async-start(), calls=%async_computation.11 | async-start | bytes 4866048 | tf_op jit(solution)/shard_map/all_gather | solution.py:243
  826.1 5.7 collective-permute-start.1
  827.8 285.5 %all-gather.14.cloned.1.call-start = ((), (), s32[]{:S(2)}) async-start(), calls=%async_computation.12 | async-start | bytes 4866048 | tf_op jit(solution)/shard_map/all_gather | solution.py:246
  832.2 1.4 collective-permute-start.2
  832.3 13.8 %copy-start.8 = (f32[3,100,768]{2,1,0:T(8,128)S(1)}, f32[3,100,768]{2,1,0:T(8,128)}, u32[]{:S(2)}) copy-start(f32[3,100,768]{2,1,0:T(8,128)} %copy-done.7) | copy-start | bytes 2764804
  834.1 9.1 collective-permute-start.3
  844.3 50.8 %collective-permute-start.4 = (bf16[16,18432]{1,0:T(8,128)(2,1)}, bf16[16,18432]{1,0:T(8,128)(2,1)S(1)}, u32[]{:S(2)}, u32[]{:S(2)}) collective-permute-start(bf16[16,18432]{1,0:T(8,128)(2,1)} %pad_maximum_fusion), channel_id=1, source_target_pairs={{0,16},{1,17},{2,18},{3,19},{4,20},{5,21},{6,22},{7,23},{8,24},{9,... | collective-permute-start | bytes 1769480 | tf_op jit(solution)/shard_map/ppermute | solution.py:24
Sparse Core Ops, SparseCore 0:
  819.2 51.9 all-gather.5
  874.0 53.1 all-gather.7
  930.0 52.9 all-gather.9
  986.2 62.5 all-gather.11
  1051.4 61.8 all-gather.13
